TPU v7x, 32 devices: a whole 2x2x4 slice. The times are simulated.
32 devices in a mesh: groups: 2 (over y), vocab: 4 (over z), edit: 2 (over x), tok: 2 (over core).
Axes of the slice: x: 2, y: 2, z: 4, core: 2. Of those that a mesh axis runs over, the one named last changes fastest.
Arguments:
- token_ids: int32 [256], P(('groups', 'tok')), parts along dimension 0, may hold values from 0 to 4095
- valid_mask: int32 [256], P(('groups', 'tok')), parts along dimension 0, may hold values 0 or 1
- key_index: int32 [4], P('groups'), parts along dimension 0, may hold values from 0 to 3
- hidden_act: bfloat16 [256, 14336], P(('groups', 'tok'), 'vocab'), parts along dimension 0, may hold values from -6 to 6
- key_table: bfloat16 [4, 14336], P(None, 'vocab'), may hold values from -0.046875 to 0.046875
- base_out: bfloat16 [256, 4096], P(('groups', 'tok'), 'vocab'), parts along dimension 0, may hold values from -50 to 50
- value_vecs: bfloat16 [4, 4096], P(('groups', 'edit'), 'vocab'), parts along dimension 0, may hold values from -6 to 6
- norm_gain: float32 [4096], replicated, may hold values from 0.5 to 1.5
- head: bfloat16 [4096, 4096], P(('vocab', 'edit')), may hold values from -46 to 46
Outputs:
- grad_value: float32 [4, 4096], P(('groups', 'edit'), 'vocab'), parts along dimension 0
- token_kl: float32 [4, 128], P(('groups', 'edit'), 'tok'), parts along dimension 0
- target_logprob: float32 [4, 128], P(('groups', 'edit'), 'tok'), parts along dimension 0
There are 2 independent parts, one for each index of `groups`. A program takes and returns all parts, laid end to end along the dimension named above; an argument that names none is the same for every part. Nothing has to cross between parts.
All inputs are finite; a program needn't handle non-finite values. No bound on the sum of `valid_mask` on one device may be relied on, other than what follows from the above.
Results may differ from a plain program's by a relative error of at most 0.0061.
Values may be sent and summed in bfloat16 or wider, within the bound.
A program may use at most 64 MiB of HBM per device.

v0:
```python
import jax
import jax.numpy as jnp
from jax import lax
from jax.sharding import PartitionSpec as P

NORM_EPS = 1e-05


def rms_scale(hidden_rows):
    return lax.rsqrt(jnp.mean(hidden_rows * hidden_rows, axis=-1, keepdims=True) + NORM_EPS)


def per_device(
    token_ids, valid_mask, key_index, hidden_act, key_table, base_out, value_vecs, norm_gain, head
):
    vocab_rows = head.shape[0]
    edit_rows = value_vecs.shape[0]
    piece_width = value_vecs.shape[1]
    key_slots = jnp.arange(key_table.shape[0], dtype=jnp.int32)
    select = (key_index[:, None] == key_slots[None, :]).astype(jnp.bfloat16)
    edit_keys = jnp.dot(select, key_table, preferred_element_type=jnp.float32).astype(jnp.bfloat16)
    coeff_part = lax.dot_general(
        edit_keys, hidden_act, (((1,), (1,)), ((), ())), preferred_element_type=jnp.float32
    )
    coeff = lax.psum(coeff_part, "vocab")
    base_rows, local_values = (
        lax.all_gather(base_out, "vocab", axis=1, tiled=True),
        lax.all_gather(value_vecs, "vocab", axis=1, tiled=True),
    )
    values = lax.all_gather(local_values, "edit", axis=0, tiled=True)
    base32 = base_rows.astype(jnp.float32)
    base_norm = (norm_gain * base32 * rms_scale(base32)).astype(jnp.bfloat16)
    base_logits = lax.dot_general(
        base_norm, head, (((1,), (1,)), ((), ())), preferred_element_type=jnp.float32
    )
    edited = base32[None, :, :] + coeff[:, :, None] * values.astype(jnp.float32)[:, None, :]
    row_scale = rms_scale(edited)
    normed = (norm_gain * edited * row_scale).astype(jnp.bfloat16)
    logits = jnp.einsum("etd,vd->etv", normed, head, preferred_element_type=jnp.float32)
    vocab_start = lax.axis_index(("vocab", "edit")) * vocab_rows
    vocab_ids = vocab_start + jnp.arange(vocab_rows, dtype=jnp.int32)
    onehot = (token_ids[:, None] == vocab_ids[None, :]).astype(jnp.float32)
    peak_base = jnp.max(base_logits, axis=-1)
    peak_edit = jnp.max(logits, axis=-1)
    peak_base, peak_edit = lax.pmax((peak_base, peak_edit), ("vocab", "edit"))
    base_exp = jnp.exp(base_logits - peak_base[:, None])
    base_total = jnp.sum(base_exp, axis=-1)
    edit_total = jnp.sum(jnp.exp(logits - peak_edit[:, :, None]), axis=-1)
    cross_sum = jnp.sum(base_exp[None, :, :] * (base_logits[None, :, :] - logits), axis=-1)
    target = jnp.sum(onehot[None, :, :] * logits, axis=-1)
    base_total, edit_total, cross_sum, target = lax.psum(
        (base_total, edit_total, cross_sum, target), ("vocab", "edit")
    )
    base_lse = peak_base + jnp.log(base_total)
    edit_lse = peak_edit + jnp.log(edit_total)
    valid = valid_mask.astype(jnp.float32)
    token_kl = valid[None, :] * (cross_sum / base_total[None, :] - base_lse[None, :] + edit_lse)
    target_logprob = target - edit_lse
    base_prob = jnp.exp(base_logits - base_lse[:, None])
    edit_prob = jnp.exp(logits - edit_lse[:, :, None])
    logit_grad = (valid[None, :, None] * (edit_prob - base_prob[None, :, :])).astype(jnp.bfloat16)
    back_rows = jnp.einsum("etv,vd->etd", logit_grad, head, preferred_element_type=jnp.float32)
    grad_y = norm_gain * back_rows
    grad_o = row_scale * grad_y - edited * row_scale**3 * jnp.mean(
        grad_y * edited, axis=-1, keepdims=True
    )
    grad_part = jnp.sum(coeff[:, :, None] * grad_o, axis=1)
    edit_start = lax.axis_index("edit") * edit_rows
    grad_total = lax.psum(grad_part, ("vocab", "edit", "tok"))
    grad_mine = lax.dynamic_slice_in_dim(grad_total, edit_start, edit_rows, 0)
    grad_piece = lax.dynamic_slice_in_dim(
        grad_mine, lax.axis_index("vocab") * piece_width, piece_width, 1
    )
    kl_mine = lax.dynamic_slice_in_dim(token_kl, edit_start, edit_rows, 0)
    target_mine = lax.dynamic_slice_in_dim(target_logprob, edit_start, edit_rows, 0)
    return (grad_piece, kl_mine, target_mine)


def solution(mesh):
    placed = (
        P(("groups", "tok")),
        P(("groups", "tok")),
        P("groups"),
        P(("groups", "tok"), "vocab"),
        P(None, "vocab"),
        P(("groups", "tok"), "vocab"),
        P(("groups", "edit"), "vocab"),
        P(),
        P(("vocab", "edit"), None),
    )
    return jax.shard_map(
        per_device,
        mesh=mesh,
        in_specs=placed,
        out_specs=(
            P(("groups", "edit"), "vocab"),
            P(("groups", "edit"), "tok"),
            P(("groups", "edit"), "tok"),
        ),
        check_vma=False,
    )
```

profile of v0, /device:TPU:0, one launch (start us, length us, event | category | flops | bytes accessed | tf_op | source)
XLA Modules:
  0.0 156.0 jit_solution(18408327459742363050)
XLA Ops:
  0.6 0.0 copy-start
  0.7 0.7 convert_element_type.32
  1.4 0.3 copy-done
  1.7 1.1 fusion.3
  2.8 13.4 %psum.42 = f32[2,64]{1,0:T(2,128)S(1)} all-reduce(f32[2,64]{1,0:T(2,128)S(1)} %fusion.3), channel_id=1, replica_groups=mesh['groups'=2,'vocab'=4,'edit'=2,'tok'=2] {'vocab'}, use_global_device_ids=true, to_apply=%region_0.0 | all-reduce | flops 128 | bytes 1024 | tf_op jit(solution)/shard_map/psum | solution.py:25
  16.3 13.3 %all_gather.10 = bf16[1,4096]{1,0:T(2,128)(2,1)S(1)} all-gather(bf16[1,1024]{1,0:T(2,128)(2,1)} %param.15), channel_id=1, replica_groups=mesh['groups'=2,'vocab'=4,'edit'=2,'tok'=2] {'vocab'}, dimensions={1}, use_global_device_ids=true | all-gather | bytes 10240 | tf_op jit(solution)/shard_map/all_gather | solution.py:28
  29.5 4.4 %all-gather = bf16[2,1,4096]{2,1,0:T(2,128)(2,1)S(1)} all-gather(bf16[1,1,4096]{2,1,0:T(2,128)(2,1)S(1)} %bitcast.20), channel_id=1, replica_groups=mesh['groups'=2,'vocab'=4,'edit'=2,'tok'=2] {'edit'}, dimensions={0}, use_global_device_ids=true | all-gather | bytes 24576 | tf_op jit(solution)/shard_map/all_gather | solution.py:30
  34.0 0.7 compare_convert_fusion
  34.7 15.0 %all_gather.9 = bf16[64,4096]{1,0:T(8,128)(2,1)S(1)} all-gather(bf16[64,1024]{1,0:T(8,128)(2,1)} %param.14), channel_id=1, replica_groups=mesh['groups'=2,'vocab'=4,'edit'=2,'tok'=2] {'vocab'}, dimensions={1}, use_global_device_ids=true | all-gather | bytes 655360 | tf_op jit(solution)/shard_map/all_gather | solution.py:27
  49.7 0.2 multiply_reduce_fusion.3
  49.9 0.0 copy-start.1
  49.9 3.9 %fusion.24 = (f32[64]{0:T(128)S(1)}, f32[64,512]{1,0:T(8,128)S(1)}) fusion(bf16[512,4096]{1,0:T(8,128)(2,1)} %param.17, f32[64]{0:T(128)S(1)} %add_rsqrt_fusion.1, f32[4096]{0:T(1024)} %param.16, bf16[64,4096]{1,0:T(8,128)(2,1)S(1)} %all_gather.9), kind=kOutput, calls=%fused_computation.48 | convolution fusion | flops 269516736 | bytes 4866560 | tf_op jit(solution)/shard_map/dot_general | solution.py:33
  53.8 0.0 copy-start.2
  53.8 0.1 convert_element_type.30
  53.9 0.4 multiply_reduce_fusion.2
  54.3 0.0 copy-done.1
  54.3 0.2 copy-done.2
  54.5 1.6 %fusion.25 = (f32[2,64]{1,0:T(2,128)S(1)}, f32[2,64,512]{2,1,0:T(8,128)S(1)}) fusion(bf16[512,4096]{1,0:T(8,128)(2,1)S(1)} %copy-done.1, f32[4096]{0:T(1024)S(1)} %copy-done.2, f32[2,64]{1,0:T(2,128)S(1)} %get-tuple-element.17, f32[2,4096]{1,0:T(2,128)S(1)} %bitcast.17, f32[64,4096]{1,0:T(8,128)S(1)} %convert_element_type.30, f32[2,64]{1,0:T(2,128)S(1)} %psum.42), kind=kOutput, calls=%fused_computation.49 | convolution fusion | flops 539557760 | bytes 5555712 | tf_op jit(solution)/shard_map/etd,vd->etv/dot_general | solution.py:39
  56.1 18.6 %all-reduce.1 = (f32[64]{0:T(128)S(1)}, f32[2,64]{1,0:T(2,128)S(1)}) all-reduce(f32[64]{0:T(128)S(1)} %get-tuple-element.18, f32[2,64]{1,0:T(2,128)S(1)} %get-tuple-element.20), channel_id=1, replica_groups=mesh['groups'=2,'vocab'=4,'edit'=2,'tok'=2] {'vocab','edit'}, use_global_device_ids=true, to_apply=%region_8.0 | all-reduce | flops 192 | bytes 1536 | tf_op jit(solution)/shard_map/pmax | solution.py:45
  74.7 0.2 fusion.23
  74.9 0.2 multiply_reduce_fusion.4
  75.1 17.7 %all-reduce = (f32[64]{0:T(128)S(1)}, f32[2,64]{1,0:T(2,128)S(1)}, f32[2,64]{1,0:T(2,128)S(1)}, f32[2,64]{1,0:T(2,128)S(1)}) all-reduce(f32[64]{0:T(128)S(1)} %get-tuple-element.14, f32[2,64]{1,0:T(2,128)S(1)} %get-tuple-element.5, ...), channel_id=1, replica_groups=mesh['groups'=2,'vocab'=4,'edit'=2,'tok'=2] {'vocab','edit'}, use_global_device_ids=true, to_apply=%region_10.0 | all-reduce | flops 448 | bytes 3584 | tf_op jit(solution)/shard_map/psum | solution.py:51
  92.8 0.1 subtract_exponential_fusion
  92.9 0.5 constant_dynamic-slice_fusion
  93.4 3.4 %multiply_reduce_fusion.1 = (f32[2,64]{1,0:T(2,128)S(1)}, f32[2,64,4096]{2,1,0:T(8,128)S(1)}) fusion(f32[2,4096]{1,0:T(2,128)S(1)} %bitcast.18, f32[64,4096]{1,0:T(8,128)S(1)} %convert_element_type.30, f32[2,64]{1,0:T(2,128)S(1)} %psum.42, bf16[512,4096]{1,0:T(8,128)(2,1)} %param.17, f32[2,64,512]{2,1,0:T(8,128)S(1)} %get-tuple-element.21, ...), kind=kOutput, calls=%fused_computation.6 | convolution fusion | flops 539754368 | bytes 7784192 | tf_op jit(solution)/shard_map/etv,vd->etd/dot_general | solution.py:62
  96.9 0.8 multiply_reduce_fusion
  97.7 57.6 %psum.45 = f32[2,4096]{1,0:T(2,128)S(1)} all-reduce(f32[2,4096]{1,0:T(2,128)S(1)} %multiply_reduce_fusion), channel_id=1, replica_groups=mesh['groups'=2,'vocab'=4,'edit'=2,'tok'=2] {'vocab','edit','tok'}, use_global_device_ids=true, to_apply=%region_13.0 | all-reduce | flops 8192 | bytes 65536 | tf_op jit(solution)/shard_map/psum | solution.py:69
  155.3 0.7 dynamic_slice.10
  (8 shorter events, 0.1 us)
Async XLA Ops:
  0.6 1.0 copy-start
  49.9 4.4 %copy-start.1 = (bf16[512,4096]{1,0:T(8,128)(2,1)S(1)}, bf16[512,4096]{1,0:T(8,128)(2,1)}, u32[]{:S(2)}) copy-start(bf16[512,4096]{1,0:T(8,128)(2,1)} %param.17) | copy-start | bytes 12582916
  53.8 0.7 copy-start.2
where the time goes:
time: 156 us
  blocking collectives  140 us (90%)
  matrix products  10 us (6%)
  other arithmetic  3.51 us (2%)
  local copies, waits for them, and re-layouts  1.73 us (1%)
    psum x1, blocking collectives, per_device(): grad_total = lax.psum(grad_part, ('vocab', 'edit', 'tok'))  57.6 us
    pmax x1, blocking collectives, per_device(): peak_base, peak_edit = lax.pmax((peak_base, peak_edit), ('vocab', 'edit'))  18.6 us
    psum x1, blocking collectives, per_device(): lax.psum((base_total, edit_total, cross_sum, target), ('vocab', 'edit'))  17.7 us
    all_gather x1, blocking collectives, per_device(): lax.all_gather(base_out, 'vocab', axis=1, tiled=True)  15 us
    psum x1, blocking collectives, per_device(): coeff = lax.psum(coeff_part, 'vocab')  13.4 us
    all_gather x1, blocking collectives, per_device(): lax.all_gather(value_vecs, 'vocab', axis=1, tiled=True)  13.3 us
    all_gather x1, blocking collectives, per_device(): values = lax.all_gather(local_values, 'edit', axis=0, tiled=True)  4.4 us
    dot_general x1, matrix products, per_device(): lax.dot_general(base_norm, head, (((1,), (1,)), ((), ())), preferred_elem...  3.87 us

commit v1 on v0

--- a/solution.py
+++ b/solution.py
@@ -66,7 +66,7 @@
     )
     grad_part = jnp.sum(coeff[:, :, None] * grad_o, axis=1)
     edit_start = lax.axis_index("edit") * edit_rows
-    grad_total = lax.psum(grad_part, ("vocab", "edit", "tok"))
+    grad_total = lax.all_gather(grad_part, ("vocab", "edit", "tok")).sum(axis=0)
     grad_mine = lax.dynamic_slice_in_dim(grad_total, edit_start, edit_rows, 0)
     grad_piece = lax.dynamic_slice_in_dim(
         grad_mine, lax.axis_index("vocab") * piece_width, piece_width, 1

time: 156 us -> 119 us (0.76)
  blocking collectives: 140 us -> 102 us
    psum x1 -> x0, blocking collectives: 57.6 us -> none  [per_device(): grad_total = lax.psum(grad_part, ('vocab', 'edit', 'tok'))]
    all_gather x0 -> x1, blocking collectives: none -> 20 us  [per_device(): grad_total = lax.all_gather(grad_part, ('vocab', 'edit', 'tok')).sum(axis=0)]
where the time goes in v1:
time: 119 us
  blocking collectives  102 us (86%)
  matrix products  10 us (8%)
  other arithmetic  3.67 us (3%)
  local copies, waits for them, and re-layouts  1.73 us (1%)
    all_gather x1, blocking collectives, per_device(): grad_total = lax.all_gather(grad_part, ('vocab', 'edit', 'tok')).sum(axis=0)  20 us
    pmax x1, blocking collectives, per_device(): peak_base, peak_edit = lax.pmax((peak_base, peak_edit), ('vocab', 'edit'))  18.6 us
    psum x1, blocking collectives, per_device(): lax.psum((base_total, edit_total, cross_sum, target), ('vocab', 'edit'))  17.7 us
    all_gather x1, blocking collectives, per_device(): lax.all_gather(base_out, 'vocab', axis=1, tiled=True)  15 us
    psum x1, blocking collectives, per_device(): coeff = lax.psum(coeff_part, 'vocab')  13.4 us
    all_gather x1, blocking collectives, per_device(): lax.all_gather(value_vecs, 'vocab', axis=1, tiled=True)  13.3 us
    all_gather x1, blocking collectives, per_device(): values = lax.all_gather(local_values, 'edit', axis=0, tiled=True)  4.4 us
    dot_general x1, matrix products, per_device(): lax.dot_general(base_norm, head, (((1,), (1,)), ((), ())), preferred_elem...  3.87 us

profile of v1, /device:TPU:0, one launch (start us, length us, event | category | flops | bytes accessed | tf_op | source)
XLA Modules:
  0.0 118.5 jit_solution(2738051936073402506)
XLA Ops:
  0.6 0.0 copy-start
  0.7 0.7 convert_element_type.32
  1.4 0.3 copy-done
  1.7 1.1 fusion.3
  2.8 13.4 %psum.35 = f32[2,64]{1,0:T(2,128)S(1)} all-reduce(f32[2,64]{1,0:T(2,128)S(1)} %fusion.3), channel_id=1, replica_groups=mesh['groups'=2,'vocab'=4,'edit'=2,'tok'=2] {'vocab'}, use_global_device_ids=true, to_apply=%region_0.0 | all-reduce | flops 128 | bytes 1024 | tf_op jit(solution)/shard_map/psum | solution.py:25
  16.3 13.3 %all_gather.16 = bf16[1,4096]{1,0:T(2,128)(2,1)S(1)} all-gather(bf16[1,1024]{1,0:T(2,128)(2,1)} %param.15), channel_id=1, replica_groups=mesh['groups'=2,'vocab'=4,'edit'=2,'tok'=2] {'vocab'}, dimensions={1}, use_global_device_ids=true | all-gather | bytes 10240 | tf_op jit(solution)/shard_map/all_gather | solution.py:28
  29.5 4.4 %all-gather.1 = bf16[2,1,4096]{2,1,0:T(2,128)(2,1)S(1)} all-gather(bf16[1,1,4096]{2,1,0:T(2,128)(2,1)S(1)} %bitcast.22), channel_id=1, replica_groups=mesh['groups'=2,'vocab'=4,'edit'=2,'tok'=2] {'edit'}, dimensions={0}, use_global_device_ids=true | all-gather | bytes 24576 | tf_op jit(solution)/shard_map/all_gather | solution.py:30
  34.0 0.7 compare_convert_fusion
  34.7 15.0 %all_gather.15 = bf16[64,4096]{1,0:T(8,128)(2,1)S(1)} all-gather(bf16[64,1024]{1,0:T(8,128)(2,1)} %param.14), channel_id=1, replica_groups=mesh['groups'=2,'vocab'=4,'edit'=2,'tok'=2] {'vocab'}, dimensions={1}, use_global_device_ids=true | all-gather | bytes 655360 | tf_op jit(solution)/shard_map/all_gather | solution.py:27
  49.7 0.2 multiply_reduce_fusion.3
  49.9 0.0 copy-start.1
  49.9 3.9 %fusion.24 = (f32[64]{0:T(128)S(1)}, f32[64,512]{1,0:T(8,128)S(1)}) fusion(bf16[512,4096]{1,0:T(8,128)(2,1)} %param.17, f32[64]{0:T(128)S(1)} %add_rsqrt_fusion.1, f32[4096]{0:T(1024)} %param.16, bf16[64,4096]{1,0:T(8,128)(2,1)S(1)} %all_gather.15), kind=kOutput, calls=%fused_computation.48 | convolution fusion | flops 269516736 | bytes 4866560 | tf_op jit(solution)/shard_map/dot_general | solution.py:33
  53.8 0.0 copy-start.2
  53.8 0.1 convert_element_type.30
  53.9 0.4 multiply_reduce_fusion.2
  54.3 0.0 copy-done.1
  54.3 0.2 copy-done.2
  54.5 1.6 %fusion.25 = (f32[2,64]{1,0:T(2,128)S(1)}, f32[2,64,512]{2,1,0:T(8,128)S(1)}) fusion(bf16[512,4096]{1,0:T(8,128)(2,1)S(1)} %copy-done.1, f32[4096]{0:T(1024)S(1)} %copy-done.2, f32[2,64]{1,0:T(2,128)S(1)} %get-tuple-element.17, f32[2,4096]{1,0:T(2,128)S(1)} %bitcast.18, f32[64,4096]{1,0:T(8,128)S(1)} %convert_element_type.30, f32[2,64]{1,0:T(2,128)S(1)} %psum.35), kind=kOutput, calls=%fused_computation.49 | convolution fusion | flops 539557760 | bytes 5555712 | tf_op jit(solution)/shard_map/etd,vd->etv/dot_general | solution.py:39
  56.1 18.6 %all-reduce.1 = (f32[64]{0:T(128)S(1)}, f32[2,64]{1,0:T(2,128)S(1)}) all-reduce(f32[64]{0:T(128)S(1)} %get-tuple-element.18, f32[2,64]{1,0:T(2,128)S(1)} %get-tuple-element.20), channel_id=1, replica_groups=mesh['groups'=2,'vocab'=4,'edit'=2,'tok'=2] {'vocab','edit'}, use_global_device_ids=true, to_apply=%region_8.0 | all-reduce | flops 192 | bytes 1536 | tf_op jit(solution)/shard_map/pmax | solution.py:45
  74.7 0.2 fusion.23
  74.9 0.2 multiply_reduce_fusion.4
  75.1 17.7 %all-reduce = (f32[64]{0:T(128)S(1)}, f32[2,64]{1,0:T(2,128)S(1)}, f32[2,64]{1,0:T(2,128)S(1)}, f32[2,64]{1,0:T(2,128)S(1)}) all-reduce(f32[64]{0:T(128)S(1)} %get-tuple-element.14, f32[2,64]{1,0:T(2,128)S(1)} %get-tuple-element.5, ...), channel_id=1, replica_groups=mesh['groups'=2,'vocab'=4,'edit'=2,'tok'=2] {'vocab','edit'}, use_global_device_ids=true, to_apply=%region_10.0 | all-reduce | flops 448 | bytes 3584 | tf_op jit(solution)/shard_map/psum | solution.py:51
  92.8 0.1 subtract_exponential_fusion
  92.9 0.5 constant_dynamic-slice_fusion
  93.4 3.4 %multiply_reduce_fusion.1 = (f32[2,64]{1,0:T(2,128)S(1)}, f32[2,64,4096]{2,1,0:T(8,128)S(1)}) fusion(f32[2,4096]{1,0:T(2,128)S(1)} %bitcast.19, f32[64,4096]{1,0:T(8,128)S(1)} %convert_element_type.30, f32[2,64]{1,0:T(2,128)S(1)} %psum.35, bf16[512,4096]{1,0:T(8,128)(2,1)} %param.17, f32[2,64,512]{2,1,0:T(8,128)S(1)} %get-tuple-element.21, ...), kind=kOutput, calls=%fused_computation.6 | convolution fusion | flops 539754368 | bytes 7784192 | tf_op jit(solution)/shard_map/etv,vd->etd/dot_general | solution.py:62
  96.9 0.8 multiply_reduce_fusion
  97.7 20.0 %all-gather.2 = f32[16,2,4096]{2,1,0:T(2,128)S(1)} all-gather(f32[1,2,4096]{2,1,0:T(2,128)S(1)} %bitcast.21), channel_id=2, replica_groups=mesh['groups'=2,'vocab'=4,'edit'=2,'tok'=2] {'vocab','edit','tok'}, dimensions={0}, use_global_device_ids=true | all-gather | bytes 557056 | tf_op jit(solution)/shard_map/all_gather | solution.py:69
  117.7 0.2 reduce_sum.87
  117.8 0.7 dynamic_slice.10
  (8 shorter events, 0.1 us)
Async XLA Ops:
  0.6 1.0 copy-start
  49.9 4.4 %copy-start.1 = (bf16[512,4096]{1,0:T(8,128)(2,1)S(1)}, bf16[512,4096]{1,0:T(8,128)(2,1)}, u32[]{:S(2)}) copy-start(bf16[512,4096]{1,0:T(8,128)(2,1)} %param.17) | copy-start | bytes 12582916
  53.8 0.7 copy-start.2
